TPU v7x, 512 devices: a whole 4x4x16 slice. The times are simulated.
512 devices in a mesh: row: 32 (over x, z_lo), col: 16 (over y, z_hi, core).
Axes of the slice: x: 4, y: 4, z: 16 (z_hi: 2, z_lo: 8; z = z_hi * 8 + z_lo), core: 2. Of those that a mesh axis runs over, the one named last changes fastest.
Arguments:
- ancestor: float32 [12288, 12288], P('row', 'col'), may hold values from -6 to 6
- pattern: int32 [96, 96], P('row', 'col'), may hold values 0 or 1
- member: int32 [96, 2], replicated, may hold values 0 or 1
- panel: float32 [12288, 512], P('col', 'row'), may hold values from -0.0546875 to 0.0546875
- diag_inv: float32 [256, 512], P(None, 'col'), may hold values from -6 to 6
Outputs:
- ancestor_panel: float32 [12288, 512], P('row', 'col')
- diag_blocks: float32 [256, 512], P(None, 'col')
All inputs are finite; a program needn't handle non-finite values. No bound on the sum of `pattern` on one device may be relied on, other than what follows from the above.
Results may differ from a plain program's by a relative error of at most 0.0001.
Values sent between devices are 32-bit elements; how exact they have to be, the bound alone decides.
No kernel may reach another device: no remote copies, remote signals or barrier semaphores. Data moves between devices by JAX's collectives and lax.ppermute only.
A program may use at most 64 MiB of HBM per device.

v0:
```python
import jax
import jax.numpy as jnp
from jax import lax
from jax.sharding import PartitionSpec as P

W = 256
BS = 128


def spread(block, axis, owner):
    block = jnp.where(lax.axis_index(axis) == owner, block, jnp.zeros_like(block))
    return lax.psum(block, axis)


def pick_member(member, start, count, which):
    rows = lax.dynamic_slice_in_dim(member, start, count, 0).astype(jnp.float32)
    return jnp.where(which == 0, rows[:, 0], rows[:, 1])


def both_terms(normed_rows, values):
    first_term = jnp.dot(
        normed_rows[:, :W].T,
        values[:, :W],
        precision=lax.Precision.HIGHEST,
        preferred_element_type=jnp.float32,
    )
    second_term = jnp.dot(
        normed_rows[:, W:].T,
        values[:, W:],
        precision=lax.Precision.HIGHEST,
        preferred_element_type=jnp.float32,
    )
    return jnp.concatenate([first_term, second_term], axis=1)


def body(ancestor, pattern, member, panel, diag_inv):
    row_count = lax.axis_size("row")
    col_count = lax.axis_size("col")
    row_idx = lax.axis_index("row")
    col_idx = lax.axis_index("col")
    row_blocks, col_blocks = pattern.shape
    local_rows, local_cols = ancestor.shape
    slice_cols = panel.shape[1]
    panel_owner = row_idx * slice_cols // W
    chosen = pick_member(member, col_idx * col_blocks, col_blocks, panel_owner)
    masked_panel = (panel.reshape(col_blocks, BS, slice_cols) * chosen[:, None, None]).reshape(
        local_cols, slice_cols
    )
    full_cols = lax.all_gather(masked_panel, "row", axis=1, tiled=True)
    weights = pattern.astype(jnp.float32)
    masked = (ancestor.reshape(row_blocks, BS, col_blocks, BS) * weights[:, None, :, None]).reshape(
        local_rows, local_cols
    )
    partial_value = jnp.dot(
        masked, full_cols, precision=lax.Precision.HIGHEST, preferred_element_type=jnp.float32
    )
    own_cols = diag_inv.shape[1]
    own_owner = col_idx * own_cols // W
    picked = pick_member(member, row_idx * row_blocks, row_blocks, own_owner)
    keep_rows = jnp.repeat(picked, BS)
    fold_ratio = row_count // col_count
    sender = lax.dynamic_slice_in_dim(full_cols, row_idx % fold_ratio * local_rows, local_rows, 0)
    summed = lax.psum_scatter(partial_value, "col", scatter_dimension=1, tiled=True)
    ancestor_panel = -(summed * keep_rows[:, None])
    normed_rows = spread(sender, "col", row_idx // fold_ratio)
    block_term = both_terms(normed_rows, partial_value)
    totals = lax.psum(block_term, ("row", "col"))
    diag_out = diag_inv + lax.dynamic_slice_in_dim(totals, col_idx * own_cols, own_cols, 1)
    return (ancestor_panel, diag_out)


def solution(mesh):
    placed = (P("row", "col"), P("row", "col"), P(), P("col", "row"), P(None, "col"))
    return jax.shard_map(
        body,
        mesh=mesh,
        in_specs=placed,
        out_specs=(P("row", "col"), P(None, "col")),
        check_vma=False,
    )
```

profile of v0, /device:TPU:2, one launch (start us, length us, event | category | flops | bytes accessed | tf_op | source)
XLA Modules:
  0.0 1086.8 jit_solution(8966737498046524540)
XLA Ops:
  7.2 0.0 copy-start.4
  7.2 0.0 all-gather.2.cloned.1.call-start
  7.2 0.8 dynamic-slice_convert_fusion.1
  8.0 0.1 broadcast_bitcast_fusion
  8.1 1.4 broadcast_multiply_fusion
  9.5 0.0 all-gather.2.cloned.1.call-update
  9.5 0.0 all-reduce.3.cloned.1.call-start
  9.6 212.4 %all-gather.2.cloned.1.call-done = f32[768,512]{0,1:T(8,128)} async-done(((f32[768,16]{0,1:T(8,128)}), f32[768,512]{0,1:T(8,128)}) %all-gather.2.cloned.1.call-update) | async-done | bytes 1572880 | tf_op jit(solution)/shard_map/all_gather | solution.py:49
  222.0 2.2 dynamic-slice_select_fusion
  224.2 0.0 all-reduce.3.cloned.1.call-update
  224.2 0.0 all-reduce.5.cloned.1.call-start
  224.2 0.0 copy-done.4
  224.3 0.2 mul.50
  224.4 0.0 copy-done.1
  224.5 1.1 copy-done
  225.6 2.2 fusion
  227.8 273.9 %all-reduce.3.cloned.1.call-done = f32[384,512]{0,1:T(8,128)} async-done(((f32[384,512]{0,1:T(8,128)}), f32[384,512]{0,1:T(8,128)}) %all-reduce.3.cloned.1.call-update) | async-done | bytes 786448 | tf_op jit(solution)/shard_map/psum | solution.py:12
  501.7 1.8 fusion.2
  503.5 1.8 fusion.5
  505.3 0.8 pad_maximum_fusion
  506.1 0.0 all-reduce.5.cloned.1.call-update
  506.2 0.0 reduce-scatter.4.cloned.1.call-start
  506.2 1.2 copy.10
  507.4 0.0 reduce-scatter.4.cloned.1.call-update
  507.4 0.1 dynamic-slice_convert_fusion
  507.5 0.1 broadcast_bitcast_fusion.1
  507.6 466.2 %all-reduce.5.cloned.1.call-done = f32[256,512]{0,1:T(8,128)} async-done(((f32[256,512]{0,1:T(8,128)}), f32[256,512]{0,1:T(8,128)}) %all-reduce.5.cloned.1.call-update) | async-done | bytes 524304 | tf_op jit(solution)/shard_map/psum | solution.py:67
  973.8 1.4 dynamic-slice_add_fusion
  975.2 103.2 %reduce-scatter.4.cloned.1.call-done = f32[32,384]{1,0:T(8,128)} async-done(((f32[512,384]{1,0:T(8,128)}), f32[32,384]{1,0:T(8,128)}) %reduce-scatter.4.cloned.1.call-update) | async-done | bytes 49168
  1078.4 0.9 copy.11
  1079.4 0.1 multiply_negate_fusion
  1079.5 0.7 copy.9
  (9 shorter events, 0.0 us)
Async XLA Ops:
  7.2 217.1 %copy-start.4 = (s32[3,6]{1,0:T(4,128)S(1)}, s32[3,6]{1,0:T(4,128)}, u32[]{:S(2)}) copy-start(s32[3,6]{1,0:T(4,128)} %param.6) | copy-start | bytes 220
  7.2 214.8 %all-gather.2.cloned.1.call-start = ((), (), s32[]{:S(2)}) async-start(), calls=%async_computation.1 | async-start | bytes 1622016 | tf_op jit(solution)/shard_map/all_gather | solution.py:49
  9.5 492.2 %all-reduce.3.cloned.1.call-start = ((), (), s32[]{:S(2)}) async-start(), calls=%async_computation.2 | async-start | bytes 1572864 | tf_op jit(solution)/shard_map/psum | solution.py:12
  222.0 2.4 copy-start.1
  224.2 1.4 copy-start
  224.2 749.6 %all-reduce.5.cloned.1.call-start = ((), (), s32[]{:S(2)}) async-start(), calls=%async_computation.3 | async-start | bytes 1048576 | tf_op jit(solution)/shard_map/psum | solution.py:67
  506.1 1.3 copy-start.3
  506.1 467.7 %copy-start.2 = (f32[256,32]{0,1:T(8,128)S(1)}, f32[256,32]{0,1:T(8,128)}, u32[]{:S(2)}) copy-start(f32[256,32]{0,1:T(8,128)} %param.9) | copy-start | bytes 98308
  506.2 572.3 %reduce-scatter.4.cloned.1.call-start = ((), (), s32[]{:S(2)}) async-start(), calls=%async_computation.4 | async-start | bytes 835584
Sparse Core Ops, SparseCore 0:
  10.6 211.3 all-gather.1
  224.9 276.7 all-reduce.2
  507.1 466.6 all-reduce.4
  978.3 100.0 reduce-scatter.3
where the time goes:
time: 1090 us
  waiting for transfers between devices  1060 us (97%)
  between operations  13.9 us (1%)
    psum x1, waiting for transfers between devices, body(): totals = lax.psum(block_term, ('row', 'col'))  466 us
    psum x1, waiting for transfers between devices, spread(): return lax.psum(block, axis)  274 us
    all_gather x1, waiting for transfers between devices, body(): full_cols = lax.all_gather(masked_panel, 'row', axis=1, tiled=True)  212 us
    unnamed x5, waiting for transfers between devices  103 us
  transfers between devices with their start and end apart: 4, of which 4 were waited for; matrix products, arithmetic and copies ran while one was open for 0% of the time, Pallas kernels for 0%

commit v1 on v0

--- a/solution.py
+++ b/solution.py
@@ -64,7 +64,8 @@
     ancestor_panel = -(summed * keep_rows[:, None])
     normed_rows = spread(sender, "col", row_idx // fold_ratio)
     block_term = both_terms(normed_rows, partial_value)
-    totals = lax.psum(block_term, ("row", "col"))
+    half = lax.psum(block_term, "row")
+    totals = lax.psum(half, "col")
     diag_out = diag_inv + lax.dynamic_slice_in_dim(totals, col_idx * own_cols, own_cols, 1)
     return (ancestor_panel, diag_out)
 

time: 1090 us -> 1330 us (1.22)
  the two profiles are of different devices: /device:TPU:2 before, /device:TPU:1 now
where the time goes in v1:
time: 1330 us
  waiting for transfers between devices  1300 us (98%)
  between operations  13.9 us (1%)
    psum x1, waiting for transfers between devices, body(): half = lax.psum(block_term, 'row')  432 us
    psum x1, waiting for transfers between devices, spread(): return lax.psum(block, axis)  278 us
    psum x1, waiting for transfers between devices, body(): totals = lax.psum(half, 'col')  251 us
    all_gather x1, waiting for transfers between devices, body(): full_cols = lax.all_gather(masked_panel, 'row', axis=1, tiled=True)  209 us
    unnamed x6, waiting for transfers between devices  129 us
  transfers between devices with their start and end apart: 5, of which 5 were waited for; matrix products, arithmetic and copies ran while one was open for 0% of the time, Pallas kernels for 0%

profile of v1, /device:TPU:1, one launch (start us, length us, event | category | flops | bytes accessed | tf_op | source)
XLA Modules:
  0.0 1329.3 jit_solution(442735773035054687)
XLA Ops:
  7.2 0.0 all-gather.2.cloned.1.call-start
  7.2 0.8 dynamic-slice_convert_fusion.1
  8.0 0.1 broadcast_bitcast_fusion
  8.1 1.4 broadcast_multiply_fusion
  9.5 0.0 all-gather.2.cloned.1.call-update
  9.5 0.0 all-reduce.4.cloned.1.call-start
  9.6 208.7 %all-gather.2.cloned.1.call-done = f32[768,512]{0,1:T(8,128)} async-done(((f32[768,16]{0,1:T(8,128)}), f32[768,512]{0,1:T(8,128)}) %all-gather.2.cloned.1.call-update) | async-done | bytes 1572880 | tf_op jit(solution)/shard_map/all_gather | solution.py:49
  218.3 2.2 dynamic-slice_select_fusion
  220.4 0.0 all-reduce.4.cloned.1.call-update
  220.5 0.0 all-reduce.6.cloned.1.call-start
  220.5 0.2 mul.50
  220.7 1.1 copy-done
  221.8 2.2 fusion
  224.0 278.2 %all-reduce.4.cloned.1.call-done = f32[384,512]{0,1:T(8,128)} async-done(((f32[384,512]{0,1:T(8,128)}), f32[384,512]{0,1:T(8,128)}) %all-reduce.4.cloned.1.call-update) | async-done | bytes 786448 | tf_op jit(solution)/shard_map/psum | solution.py:12
  502.2 1.8 fusion.2
  504.0 1.8 fusion.5
  505.8 0.8 pad_maximum_fusion
  506.7 0.0 all-reduce.6.cloned.1.call-update
  506.7 0.0 reduce-scatter.4.cloned.1.call-start
  506.7 1.2 copy.10
  507.9 0.0 reduce-scatter.4.cloned.1.call-update
  507.9 0.0 all-reduce.8.cloned.1.call-start
  508.0 0.1 dynamic-slice_convert_fusion
  508.1 432.0 %all-reduce.6.cloned.1.call-done = f32[256,512]{0,1:T(8,128)} async-done(((f32[256,512]{0,1:T(8,128)}), f32[256,512]{0,1:T(8,128)}) %all-reduce.6.cloned.1.call-update) | async-done | bytes 524304 | tf_op jit(solution)/shard_map/psum | solution.py:67
  940.1 0.0 all-reduce.8.cloned.1.call-update
  940.1 0.1 broadcast_bitcast_fusion.1
  940.2 128.4 %reduce-scatter.4.cloned.1.call-done = f32[32,384]{1,0:T(8,128)} async-done(((f32[512,384]{1,0:T(8,128)}), f32[32,384]{1,0:T(8,128)}) %reduce-scatter.4.cloned.1.call-update) | async-done | bytes 49168
  1068.6 0.9 copy.11
  1069.6 0.1 multiply_negate_fusion
  1069.7 0.7 copy.9
  1070.4 250.9 %all-reduce.8.cloned.1.call-done = f32[256,512]{0,1:T(8,128)} async-done(((f32[256,512]{0,1:T(8,128)}), f32[256,512]{0,1:T(8,128)}) %all-reduce.8.cloned.1.call-update) | async-done | bytes 524304 | tf_op jit(solution)/shard_map/psum | solution.py:68
  1321.4 1.4 dynamic-slice_add_fusion
  (12 shorter events, 0.0 us)
Async XLA Ops:
  7.2 213.3 %copy-start.4 = (s32[3,6]{1,0:T(4,128)S(1)}, s32[3,6]{1,0:T(4,128)}, u32[]{:S(2)}) copy-start(s32[3,6]{1,0:T(4,128)} %param.6) | copy-start | bytes 220
  7.2 211.1 %all-gather.2.cloned.1.call-start = ((), (), s32[]{:S(2)}) async-start(), calls=%async_computation.1 | async-start | bytes 1622016 | tf_op jit(solution)/shard_map/all_gather | solution.py:49
  9.5 492.7 %all-reduce.4.cloned.1.call-start = ((), (), s32[]{:S(2)}) async-start(), calls=%async_computation.2 | async-start | bytes 1572864 | tf_op jit(solution)/shard_map/psum | solution.py:12
  218.3 2.4 copy-start.1
  220.4 1.4 copy-start
  220.5 719.6 %all-reduce.6.cloned.1.call-start = ((), (), s32[]{:S(2)}) async-start(), calls=%async_computation.3 | async-start | bytes 1048576 | tf_op jit(solution)/shard_map/psum | solution.py:67
  506.7 1.3 copy-start.3
  506.7 814.7 %copy-start.2 = (f32[256,32]{0,1:T(8,128)S(1)}, f32[256,32]{0,1:T(8,128)}, u32[]{:S(2)}) copy-start(f32[256,32]{0,1:T(8,128)} %param.9) | copy-start | bytes 98308
  506.7 562.0 %reduce-scatter.4.cloned.1.call-start = ((), (), s32[]{:S(2)}) async-start(), calls=%async_computation.5 | async-start | bytes 835584
  507.9 813.4 %all-reduce.8.cloned.1.call-start = ((), (), s32[]{:S(2)}) async-start(), calls=%async_computation.4 | async-start | bytes 1048576 | tf_op jit(solution)/shard_map/psum | solution.py:68
Sparse Core Ops, SparseCore 0:
  10.6 207.5 all-gather.1
  221.2 281.0 all-reduce.3
  506.8 433.2 all-reduce.5
  944.6 124.0 reduce-scatter.3
  1071.4 249.9 all-reduce.7
